TPU v7x, 32 devices: a whole 2x2x4 slice. The times are simulated.
32 devices in a mesh: gx: 4 (over y, x), gy: 8 (over z, core).
Axes of the slice: x: 2, y: 2, z: 4, core: 2. Of those that a mesh axis runs over, the one named last changes fastest.
Arguments:
- old_state: float32 [8, 8, 128, 1024], P(None, None, 'gx', 'gy'), may hold values from -6 to 6
- section_prims: float32 [8, 8, 128, 1024], P(None, None, 'gx', 'gy'), may hold values from -3 to 3, as said below
- shear_whole: int32 [1], replicated, may hold values from 0 to 1023
- shear_frac: float32 [1], replicated, may hold values from 0 to 1
Outputs:
- new_state: float32 [8, 8, 128, 1024], P(None, None, 'gx', 'gy')
Inputs may be any that keep to these rules, and one draw needn't show every extreme that they name: section_prims holds density in [0.5, 2] in field 0 and pressure in [0.3, 3] in field 4; the other fields lie in the stated range.
All inputs are finite; a program needn't handle non-finite values.
Results may differ from a plain program's by a relative error of at most 0.0003.
Values sent between devices are 32-bit elements; how exact they have to be, the bound alone decides.
No kernel may reach another device: no remote copies, remote signals or barrier semaphores. Data moves between devices by JAX's collectives and lax.ppermute only.
A program may use at most 128 MiB of HBM per device.

v0:
```python
import functools

import jax
import jax.numpy as jnp
from jax import lax
from jax.experimental import pallas as pl
from jax.experimental.pallas import tpu as pltpu
from jax.sharding import PartitionSpec as P

gamma_gas = 5.0 / 3.0
omega_rate = 1.0
shear_rate = 1.5
time_step = 0.1

FIELDS = 8
EDGE = 8
ROWS = 128 // EDGE


def median0(a, b):
    return jnp.maximum(jnp.minimum(a, b), jnp.minimum(jnp.maximum(a, b), 0.0))


def half_slope(a, b):
    return 0.5 * median0(a, b)


def side(w, n):
    t, u = (n + 1) % 3, (n + 2) % 3
    rho, p = w[0], w[4]
    vn, vt, vu = w[1 + n], w[1 + t], w[1 + u]
    bn, bt, bu = w[5 + n], w[5 + t], w[5 + u]
    mn, mt, mu = rho * vn, rho * vt, rho * vu
    mnvn = mn * vn
    bn2 = bn * bn
    bt2 = bt * bt + bu * bu
    bsq = bn2 + bt2
    q = 0.5 * (mnvn + mt * vt + mu * vu) + p * (1.0 / (gamma_gas - 1.0))
    pm = 0.5 * bsq
    cons = [None] * FIELDS
    flux = [None] * FIELDS
    cons[0], cons[1 + n], cons[1 + t], cons[1 + u] = rho, mn, mt, mu
    cons[4] = q + pm
    cons[5 + n], cons[5 + t], cons[5 + u] = bn, bt, bu
    flux[0] = mn
    flux[1 + n] = mnvn + (p + pm - bn2)
    flux[1 + t] = mt * vn - bt * bn
    flux[1 + u] = mu * vn - bu * bn
    flux[4] = (q + p + bt2) * vn - bn * (vt * bt + vu * bu)
    flux[5 + t] = bt * vn - vt * bn
    flux[5 + u] = bu * vn - vu * bn
    a = (0.5 * gamma_gas) * p
    diff = a - pm
    disc = diff * diff + a * (bt2 + bt2)
    x = a + pm + disc * lax.rsqrt(jnp.maximum(disc, 1e-30))
    speed = jnp.abs(vn) + x * lax.rsqrt(rho * x)
    return cons, flux, speed


def twice_face(left, right, n):
    cl, fl, sl = side(left, n)
    cr, fr, sr = side(right, n)
    s = jnp.maximum(sl, sr)
    out = []
    for j in range(FIELDS):
        jump = s * (cr[j] - cl[j])
        out.append(-jump if j == 5 + n else fl[j] + fr[j] - jump)
    return out


def lanes():
    return lax.broadcasted_iota(jnp.int32, (8, 128), 1)


def rows_of(ref, x):
    return [ref[f, x] for f in range(FIELDS)]


def transposing(src, dst, sem):
    return [
        [pltpu.make_async_copy(src.at[f, z], dst.at[f, :, z], sem.at[f, z]) for z in range(8)]
        for f in range(FIELDS)
    ]


def pack_kernel(nx, w_ref, wt_ref, xa_ref, own_ref, ex_ref, sem):
    copies = transposing(w_ref, wt_ref, sem)
    for field in copies:
        for copy in field:
            copy.start()
    odd = lax.rem(lax.axis_index("gx"), 2)
    first_a = (1 - odd) * (nx - 2)
    first_b = odd * (nx - 2)
    lane = lanes()
    group, place = lane // EDGE, lax.rem(lane, EDGE)
    middle = (place > 1) & (place < 6)
    for f in range(FIELDS):
        for copy in copies[f]:
            copy.wait()
        for g in range(2):
            xa_ref[f, g] = wt_ref[f, first_a + g]
            ex_ref[f, g] = wt_ref[f, first_b + g]
        tiles = []
        for v in range(nx // ROWS):
            acc = jnp.zeros((8, 128), jnp.float32)
            for i in range(ROWS):
                row = wt_ref[f, v * ROWS + i]
                acc = jnp.where(group == i, pltpu.roll(row, (EDGE * i + 4) % 128, 1), acc)
            own_ref[f, v] = acc
            tiles.append(acc)
        for v in range(0, len(tiles), 2):
            ex_ref[f, 2 + v // 2] = jnp.where(middle, tiles[v], pltpu.roll(tiles[v + 1], 4, 1))


def shear_kernel(whole_ref, frac_ref, ex_ref, c_ref, y_ref, xb_ref):
    gx, odd_y = lax.axis_index("gx"), lax.rem(lax.axis_index("gy"), 2)
    upper = gx == lax.axis_size("gx") - 1
    end = upper | (gx == 0)
    shift = jnp.where(end, lax.rem(whole_ref[0], 128), 0)
    frac = jnp.where(end, frac_ref[0], 0.0)
    sibling = (odd_y == 1) != upper
    lane = lanes()

    def window(own, other, s):
        amount = jnp.where(upper, lax.rem(128 - s, 128), lax.rem(s, 128))
        low = jnp.where(upper, 0, s)
        high = jnp.where(upper, 128 - s, 128)
        near = (lane >= low) & (lane < high)
        return pltpu.roll(own, amount, 1), pltpu.roll(other, amount, 1), near

    for f in range(FIELDS):
        for g in range(2):
            own = ex_ref[f, g]
            other = jnp.where(sibling, c_ref[f, g], y_ref[f, g])
            a, b, near = window(own, other, shift)
            first = jnp.where(near, a, b)
            a, b, near = window(own, other, shift + 1)
            second = jnp.where(near, a, b)
            xb_ref[f, g] = (1.0 - frac) * first + frac * second


def inner_kernel(
    nx, wt_ref, old_ref, acc_ref, old_t, g_ref, l_ref, d_ref, al_ref, am_ref, ar_ref, ag_ref, sem
):
    copies = [copy for field in transposing(old_ref, old_t, sem) for copy in field]
    for copy in copies:
        copy.start()
    lane = lanes()
    whole = (lane > 0) & (lane < 126)

    def finish(x, w, div):
        rho, vx, vy, vz, p, bx, by, bz = w
        mx, my, mz = rho * vx, rho * vy, rho * vz
        energy = (
            p * (1.0 / (gamma_gas - 1.0))
            + 0.5 * (mx * vx + my * vy + mz * vz)
            + 0.5 * (bx * bx + by * by + bz * bz)
        )
        cons = [rho, mx, my, mz, energy, bx, by, bz]
        src = [None] * FIELDS
        src[1] = (time_step * 2.0 * omega_rate) * my
        src[2] = (-time_step * (2.0 - shear_rate) * omega_rate) * mx
        src[4] = (time_step * shear_rate * omega_rate) * (mx * vy - bx * by)
        src[6] = (-time_step * shear_rate * omega_rate) * bx
        for f in range(FIELDS):
            total = cons[f] + (0.5 * time_step) * div[f]
            acc_ref[f, x] = total if src[f] is None else total + src[f]

    def vertical(w):
        left, right = [], []
        for f in range(FIELDS):
            up = pltpu.roll(w[f], 7, 0) - w[f]
            h = half_slope(pltpu.roll(up, 1, 0), up)
            left.append(w[f] + h)
            right.append(pltpu.roll(w[f] - h, 7, 0))
        g = twice_face(left, right, 2)
        return [pltpu.roll(v, 1, 0) - v for v in g]

    def radial(x):
        w2 = rows_of(wt_ref, jnp.minimum(x + 1, nx - 1))
        w3 = rows_of(wt_ref, jnp.minimum(x + 2, nx - 1))
        left, right = [], []
        for f in range(FIELDS):
            step = w3[f] - w2[f]
            h = half_slope(d_ref[f], step)
            left.append(l_ref[f])
            right.append(w2[f] - h)
            l_ref[f] = w2[f] + h
            d_ref[f] = step
        keep = jnp.where((x > 0) & (x < nx - 2), 1.0, 0.0)
        return [keep * v for v in twice_face(left, right, 0)]

    def states(x):
        for f in range(FIELDS):
            w = wt_ref[f, x]
            h = half_slope(w - pltpu.roll(w, 1, 1), pltpu.roll(w, 127, 1) - w)
            al_ref[f, x] = w + h
            am_ref[f, x] = w - h

    def turn(x):
        for f in range(FIELDS):
            ar_ref[f, x] = pltpu.roll(am_ref[f, x], 127, 1)

    def faces(x):
        g = twice_face(rows_of(al_ref, x), rows_of(ar_ref, x), 1)
        for f in range(FIELDS):
            ag_ref[f, x] = jnp.where(whole, g[f], 0.0)

    states(0)
    states(1)
    states(2)
    turn(0)
    turn(1)
    faces(0)
    for f in range(FIELDS):
        g_ref[f] = jnp.zeros((8, 128), jnp.float32)
        l_ref[f] = wt_ref[f, 0]
        d_ref[f] = wt_ref[f, 1] - wt_ref[f, 0]

    def body(x, _):
        w = rows_of(wt_ref, x)
        along = rows_of(ag_ref, x)
        along = [pltpu.roll(v, 1, 1) - v for v in along]
        faces(jnp.minimum(x + 1, nx - 1))
        turn(jnp.minimum(x + 2, nx - 1))
        states(jnp.minimum(x + 3, nx - 1))
        div = vertical(w)
        g = radial(x)
        for f in range(FIELDS):
            div[f] = div[f] + (g_ref[f] - g[f]) + along[f]
            g_ref[f] = g[f]
        finish(x, w, div)
        return 0

    lax.fori_loop(0, nx, body, 0)
    for copy in copies:
        copy.wait()

    def add(x, _):
        for f in range(FIELDS):
            acc_ref[f, x] = 0.5 * (acc_ref[f, x] + old_t[f, x])
        return 0

    lax.fori_loop(0, nx, add, 0)


def outer_kernel(
    nx, wt_ref, acc_ref, own_ref, c_ref, y_ref, xa_ref, xb_hbm, out_ref,
    new_ref, q_ref, d_ref, xb_ref, sem, xb_sem,
):
    fetch = pltpu.make_async_copy(xb_hbm, xb_ref, xb_sem)
    fetch.start()
    odd_x, odd_y = lax.rem(lax.axis_index("gx"), 2), lax.rem(lax.axis_index("gy"), 2)
    lane = lanes()
    scale = 0.25 * time_step

    place = lax.rem(lane, EDGE)
    low = place < 4
    for v in range(nx // ROWS):
        left, right = [], []
        for f in range(FIELDS):
            own, core, cross = own_ref[f, v], c_ref[f, 2 + v // 2], y_ref[f, 2 + v // 2]
            before = jnp.where(odd_y == 1, core, cross)
            after = jnp.where(odd_y == 1, cross, core)
            if v % 2:
                before, after = pltpu.roll(before, 124, 1), pltpu.roll(after, 124, 1)
            end = jnp.where(low, own, after)
            start = jnp.where(low, before, own)
            w0 = jnp.where(low, pltpu.roll(end, 1, 1), pltpu.roll(start, 2, 1))
            w1 = jnp.where(low, end, pltpu.roll(start, 1, 1))
            w2 = jnp.where(low, pltpu.roll(end, 127, 1), start)
            w3 = jnp.where(low, pltpu.roll(end, 126, 1), pltpu.roll(start, 127, 1))
            mid = w2 - w1
            left.append(w1 + half_slope(w1 - w0, mid))
            right.append(w2 - half_slope(mid, w3 - w2))
        g = twice_face(left, right, 1)
        for f in range(FIELDS):
            lower = jnp.where(low, jnp.where(place == 3, pltpu.roll(g[f], 1, 1), 0.0), g[f])
            upper = jnp.where(low, g[f], jnp.where(place == 4, pltpu.roll(g[f], 127, 1), 0.0))
            q_ref[f, v] = scale * (lower - upper)

    fetch.wait()

    def ghosts(i):
        above = (odd_x == 1) != (i < 2)
        return [jnp.where(above, xb_ref[f, i % 2], xa_ref[f, i % 2]) for f in range(FIELDS)]

    def rows(x):
        return rows_of(wt_ref, x)

    def radial(w0, w1, w2, w3):
        left, right = [], []
        for f in range(FIELDS):
            mid = w2[f] - w1[f]
            left.append(w1[f] + half_slope(w1[f] - w0[f], mid))
            right.append(w2[f] - half_slope(mid, w3[f] - w2[f]))
        return twice_face(left, right, 0)

    g0 = radial(ghosts(0), ghosts(1), rows(0), rows(1))
    g1 = radial(ghosts(1), rows(0), rows(1), rows(2))
    for f in range(FIELDS):
        d_ref[f, 0] = scale * (g0[f] - g1[f])
        d_ref[f, 1] = scale * g1[f]
    g0 = radial(rows(nx - 3), rows(nx - 2), rows(nx - 1), ghosts(2))
    g1 = radial(rows(nx - 2), rows(nx - 1), ghosts(2), ghosts(3))
    for f in range(FIELDS):
        d_ref[f, 2] = -scale * g0[f]
        d_ref[f, 3] = scale * (g0[f] - g1[f])

    edge = (lane < 2) | (lane > 125)
    copies = []
    for f in range(FIELDS):
        for x in range(nx):
            q = pltpu.roll(q_ref[f, x // ROWS], (124 - EDGE * (x % ROWS)) % 128, 1)
            new = acc_ref[f, x] + jnp.where(edge, q, 0.0)
            at = {0: 0, 1: 1, nx - 2: 2, nx - 1: 3}.get(x)
            new_ref[f, x] = new if at is None else new + d_ref[f, at]
        for z in range(8):
            copy = pltpu.make_async_copy(new_ref.at[f, :, z], out_ref.at[f, z], sem.at[f, z])
            copy.start()
            copies.append(copy)
    for copy in copies:
        copy.wait()


def swaps(nx, ny):
    def at(g, j):
        return (g % nx) * ny + j % ny

    grid = [(g, j) for g in range(nx) for j in range(ny)]
    core = [(at(g, j), at(g, j ^ 1)) for g, j in grid]
    cross = [(at(g, j), at(g, j + 1 if j % 2 else j - 1)) for g, j in grid]
    along = [(at(g, j), at(g ^ 1, j)) for g, j in grid]

    def ends(k):
        there = [(at(0, j), at(nx - 1, j + k)) for j in range(ny)]
        return there + [(b, a) for a, b in there]

    def other(k):
        inside = [(at(g, j), at(g + 1 if g % 2 else g - 1, j)) for g, j in grid if 0 < g < nx - 1]
        return inside + ends(k)

    return core, cross, along, other


def on_device(old_state, section_prims, shear_whole, shear_frac):
    n_gx, n_gy = lax.axis_size("gx"), lax.axis_size("gy")
    gx, gy = lax.axis_index("gx"), lax.axis_index("gy")
    fields, nz, nx, cells = section_prims.shape
    assert (fields, nz, cells) == (FIELDS, 8, 128)
    assert nx % (2 * ROWS) == 0 and n_gx % 2 == 0 and n_gy % 2 == 0
    axes = ("gx", "gy")
    core, cross, along, other = swaps(n_gx, n_gy)
    f32 = jnp.float32
    vmem = pl.BlockSpec(memory_space=pltpu.VMEM)
    smem = pl.BlockSpec(memory_space=pltpu.SMEM)
    hbm = pl.BlockSpec(memory_space=pltpu.HBM)
    block = (fields, nx, nz, cells)
    tile = (fields, nz, cells)
    tiles = nx // ROWS
    edge_rows = jax.ShapeDtypeStruct((fields, 2, nz, cells), f32)

    def room(mib):
        return pltpu.CompilerParams(vmem_limit_bytes=mib << 20)

    w, old = (pltpu.with_memory_space_constraint(v, pltpu.HBM) for v in (section_prims, old_state))
    wt, xa, own, ex = pl.pallas_call(
        functools.partial(pack_kernel, nx),
        out_shape=(
            jax.ShapeDtypeStruct(block, f32),
            edge_rows,
            jax.ShapeDtypeStruct((fields, tiles, nz, cells), f32),
            jax.ShapeDtypeStruct((fields, 2 + tiles // 2, nz, cells), f32),
        ),
        in_specs=[hbm],
        out_specs=(vmem,) * 4,
        scratch_shapes=[pltpu.SemaphoreType.DMA((fields, nz))],
        compiler_params=room(8),
        name="pack",
    )(w)

    c_in = lax.ppermute(ex, axes, core)
    y_in = lax.ppermute(ex, axes, cross)
    xa_in = lax.ppermute(xa, axes, along)
    xb = pl.pallas_call(
        shear_kernel,
        out_shape=edge_rows,
        in_specs=[smem, smem, vmem, vmem, vmem],
        out_specs=vmem,
        compiler_params=room(8),
        name="shear",
    )(shear_whole, shear_frac, ex, c_in, y_in)

    def branch(k):
        def run(xb, wt, old):
            xb_in = lax.ppermute(xb, axes, other(k))
            acc = pl.pallas_call(
                functools.partial(inner_kernel, nx),
                out_shape=jax.ShapeDtypeStruct(block, f32),
                in_specs=[vmem, hbm],
                out_specs=vmem,
                scratch_shapes=[pltpu.VMEM(block, f32)]
                + [pltpu.VMEM(tile, f32)] * 3
                + [pltpu.VMEM(block, f32)] * 4
                + [pltpu.SemaphoreType.DMA((fields, nz))],
                compiler_params=room(16),
                cost_estimate=pl.CostEstimate(
                    flops=720 * nx * nz * cells, bytes_accessed=12 * fields * nx * nz * cells, transcendentals=0
                ),
                name="inner",
            )(wt, old)
            return xb_in, acc

        return run

    whole = lax.shift_right_logical(shear_whole[0], 7)
    xb_in, acc = lax.switch(whole, [branch(k) for k in range(n_gy)], xb, wt, old)

    return pl.pallas_call(
        functools.partial(outer_kernel, nx),
        out_shape=jax.ShapeDtypeStruct(section_prims.shape, f32),
        in_specs=[vmem] * 6 + [hbm],
        out_specs=hbm,
        scratch_shapes=[
            pltpu.VMEM(block, f32),
            pltpu.VMEM((fields, tiles, nz, cells), f32),
            pltpu.VMEM((fields, 4, nz, cells), f32),
            pltpu.VMEM((fields, 2, nz, cells), f32),
            pltpu.SemaphoreType.DMA((fields, nz)),
            pltpu.SemaphoreType.DMA,
        ],
        compiler_params=room(12),
        name="outer",
    )(wt, acc, own, c_in, y_in, xa_in, xb_in)


def solution(mesh):
    in_specs = (P(None, None, "gx", "gy"), P(None, None, "gx", "gy"), P(), P())
    out_specs = P(None, None, "gx", "gy")
    return jax.shard_map(
        on_device, mesh=mesh, in_specs=in_specs, out_specs=out_specs, check_vma=False
    )
```

profile of v0, /device:TPU:0, one launch (start us, length us, event | category | flops | bytes accessed | tf_op | source)
XLA Modules:
  0.0 21.3 jit_solution(13830970386991540687)
XLA Ops:
  0.0 2.7 %pack.1 = (f32[8,32,8,128]{3,2,1,0:T(8,128)S(1)}, f32[8,2,8,128]{3,2,1,0:T(8,128)S(1)}, f32[8,2,8,128]{3,2,1,0:T(8,128)S(1)}, f32[8,3,8,128]{3,2,1,0:T(8,128)S(1)}) custom-call(f32[8,8,32,128]{3,2,1,0:T(8,128)} %w_ref.1), custom_call_target="tpu_custom_call" | custom-call | tf_op jit(solution)/shard_map/pack/pallas_call | solution.py:367
  2.7 4.6 %collective-permute-start.9 = (f32[8,3,8,128]{3,2,1,0:T(8,128)S(1)}, f32[8,3,8,128]{3,2,1,0:T(8,128)S(1)}, u32[]{:S(2)}, u32[]{:S(2)}) collective-permute-start(f32[8,3,8,128]{3,2,1,0:T(8,128)S(1)} %get-tuple-element.84.ex_ref), channel_id=1, source_target_pairs={{0,7},{1,2},{2,1},{3,4},{4,3},{5,6},{6,5},{7,0},{8,15},{9,10},{10,... | collective-permute-start | bytes 294920 | tf_op jit(solution)/shard_map/ppermute | solution.py:383
  7.3 0.0 collective-permute-start.8
  7.3 1.5 %collective-permute-start.10 = (f32[8,2,8,128]{3,2,1,0:T(8,128)S(1)}, f32[8,2,8,128]{3,2,1,0:T(8,128)S(1)}, u32[]{:S(2)}, u32[]{:S(2)}) collective-permute-start(f32[8,2,8,128]{3,2,1,0:T(8,128)S(1)} %get-tuple-element.87), channel_id=1, source_target_pairs={{0,8},{1,9},{2,10},{3,11},{4,12},{5,13},{6,14},{7,15},{8,0},{9,1},... | collective-permute-start | bytes 196616 | tf_op jit(solution)/shard_map/ppermute | solution.py:384
  10.1 0.0 collective-permute-done.9.y_ref
  10.1 0.0 collective-permute-done.8.c_ref
  10.1 0.2 shear.1
  10.3 8.5 %conditional.1 = (f32[8,2,8,128]{3,2,1,0:T(8,128)}, f32[8,32,8,128]{3,2,1,0:T(8,128)S(1)}) conditional(s32[]{:T(128)} %bitcast, (f32[8,2,8,128]{3,2,1,0:T(8,128)S(1)}, f32[8,32,8,128]{3,2,1,0:T(8,128)S(1)}, f32[8,8,32,128]{3,2,1,0:T(8,128)}) %tuple.37, (f32[8,2,8,128]{3,2,1,0:T(8,128)S(1)}, ...), branch_computations={%region_0.0_spmd, %region_1.0_spmd, %region_2.0_spmd, %region_3.0_... | conditional | flops 23592960 | bytes 3407928 | solution.py:417
  10.3 3.3 %collective-permute-start = (f32[8,2,8,128]{3,2,1,0:T(8,128)S(1)}, f32[8,2,8,128]{3,2,1,0:T(8,128)}, u32[]{:S(2)}, u32[]{:S(2)}) collective-permute-start(f32[8,2,8,128]{3,2,1,0:T(8,128)S(1)} %get-tuple-element.53), channel_id=1, source_target_pairs={{8,16},{9,17},{10,18},{11,19},{12,20},{13,21},{14,22},{15,23},{16,... | collective-permute-start | bytes 196616 | tf_op jit(solution)/shard_map/cond/branch_0_fun/ppermute | solution.py:396
  13.6 5.1 %inner.8 = f32[8,32,8,128]{3,2,1,0:T(8,128)S(1)} custom-call(f32[8,32,8,128]{3,2,1,0:T(8,128)S(1)} %get-tuple-element.54.wt_ref, f32[8,8,32,128]{3,2,1,0:T(8,128)} %get-tuple-element.55.old_ref), custom_call_target="tpu_custom_call" | custom-call | flops 23592960 | bytes 3145728 | tf_op jit(solution)/shard_map/cond/branch_0_fun/inner/pallas_call | solution.py:397
  18.7 0.0 collective-permute-done
  18.7 0.0 collective-permute-done.10.xa_ref
  18.7 2.6 %outer.1 = f32[8,8,32,128]{3,2,1,0:T(8,128)} custom-call(f32[8,32,8,128]{3,2,1,0:T(8,128)S(1)} %get-tuple-element.83.wt_ref, f32[8,32,8,128]{3,2,1,0:T(8,128)S(1)} %get-tuple-element.85.acc_ref, f32[8,2,8,128]{3,2,1,0:T(8,128)S(1)} %get-tuple-element.86.own_ref, f32[8,3,8,128]{3,2,1,0:T(8,128)S(1)} %collective-permute-done.8.c_ref, ...), custom_call_target="tpu_custom_call" | custom-call | tf_op jit(solution)/shard_map/outer/pallas_call | solution.py:419
Async XLA Ops:
  2.7 7.4 %collective-permute-start.9 = (f32[8,3,8,128]{3,2,1,0:T(8,128)S(1)}, f32[8,3,8,128]{3,2,1,0:T(8,128)S(1)}, u32[]{:S(2)}, u32[]{:S(2)}) collective-permute-start(f32[8,3,8,128]{3,2,1,0:T(8,128)S(1)} %get-tuple-element.84.ex_ref), channel_id=1, source_target_pairs={{0,7},{1,2},{2,1},{3,4},{4,3},{5,6},{6,5},{7,0},{8,15},{9,10},{10,... | collective-permute-start | bytes 294920 | tf_op jit(solution)/shard_map/ppermute | solution.py:383
  7.3 2.8 %collective-permute-start.8 = (f32[8,3,8,128]{3,2,1,0:T(8,128)S(1)}, f32[8,3,8,128]{3,2,1,0:T(8,128)S(1)}, u32[]{:S(2)}, u32[]{:S(2)}) collective-permute-start(f32[8,3,8,128]{3,2,1,0:T(8,128)S(1)} %get-tuple-element.84.ex_ref), channel_id=1, source_target_pairs={{0,1},{1,0},{2,3},{3,2},{4,5},{5,4},{6,7},{7,6},{8,9},{9,8},{10,11... | collective-permute-start | bytes 294920 | tf_op jit(solution)/shard_map/ppermute | solution.py:382
  7.3 11.5 %collective-permute-start.10 = (f32[8,2,8,128]{3,2,1,0:T(8,128)S(1)}, f32[8,2,8,128]{3,2,1,0:T(8,128)S(1)}, u32[]{:S(2)}, u32[]{:S(2)}) collective-permute-start(f32[8,2,8,128]{3,2,1,0:T(8,128)S(1)} %get-tuple-element.87), channel_id=1, source_target_pairs={{0,8},{1,9},{2,10},{3,11},{4,12},{5,13},{6,14},{7,15},{8,0},{9,1},... | collective-permute-start | bytes 196616 | tf_op jit(solution)/shard_map/ppermute | solution.py:384
  10.3 8.4 %collective-permute-start = (f32[8,2,8,128]{3,2,1,0:T(8,128)S(1)}, f32[8,2,8,128]{3,2,1,0:T(8,128)}, u32[]{:S(2)}, u32[]{:S(2)}) collective-permute-start(f32[8,2,8,128]{3,2,1,0:T(8,128)S(1)} %get-tuple-element.53), channel_id=1, source_target_pairs={{8,16},{9,17},{10,18},{11,19},{12,20},{13,21},{14,22},{15,23},{16,... | collective-permute-start | bytes 196616 | tf_op jit(solution)/shard_map/cond/branch_0_fun/ppermute | solution.py:396
where the time goes:
time: 21 us; the launch traced here: 21.3 us
  Pallas kernels  10.6 us (50%)
  starting transfers between devices  9.32 us (44%)
  between operations  1.35 us (6%)
    pallas_call x1, Pallas kernels, run(): pl.pallas_call(functools.partial(inner_kernel, nx), out_shape=jax.ShapeDt...  5.14 us
    ppermute x1, starting transfers between devices, on_device(): y_in = lax.ppermute(ex, axes, cross)  4.55 us
    ppermute x1, starting transfers between devices, run(): xb_in = lax.ppermute(xb, axes, other(k))  3.28 us
    pallas_call x1, Pallas kernels, on_device(): pl.pallas_call(functools.partial(pack_kernel, nx), out_shape=(jax.ShapeDt...  2.72 us
    pallas_call x1, Pallas kernels, on_device(): pl.pallas_call(functools.partial(outer_kernel, nx), out_shape=jax.ShapeDt...  2.59 us
    ppermute x1, starting transfers between devices, on_device(): xa_in = lax.ppermute(xa, axes, along)  1.49 us
  transfers between devices with their start and end apart: 4, of which 0 were waited for; matrix products, arithmetic and copies ran while one was open for 0% of the time, Pallas kernels for 25%

commit v1 on v0

--- a/solution.py
+++ b/solution.py
@@ -15,6 +15,7 @@
 FIELDS = 8
 EDGE = 8
 ROWS = 128 // EDGE
+UNROLL = 2
 
 
 def median0(a, b):
@@ -76,17 +77,65 @@
     return [ref[f, x] for f in range(FIELDS)]
 
 
-def transposing(src, dst, sem):
+def transposing(src, dst, sem, parts):
+    n = FIELDS // parts
     return [
-        [pltpu.make_async_copy(src.at[f, z], dst.at[f, :, z], sem.at[f, z]) for z in range(8)]
-        for f in range(FIELDS)
+        [
+            pltpu.make_async_copy(
+                src.at[n * i : n * i + n, z], dst.at[n * i : n * i + n, :, z], sem.at[i, z]
+            )
+            for z in range(8)
+        ]
+        for i in range(parts)
     ]
 
 
-def pack_kernel(nx, w_ref, wt_ref, xa_ref, own_ref, ex_ref, sem):
-    copies = transposing(w_ref, wt_ref, sem)
-    for field in copies:
-        for copy in field:
+def upright(nx, wt_ref, acc_ref):
+    def body(x, _):
+        w = rows_of(wt_ref, x)
+        left, right = [], []
+        for f in range(FIELDS):
+            up = pltpu.roll(w[f], 7, 0) - w[f]
+            h = half_slope(pltpu.roll(up, 1, 0), up)
+            left.append(w[f] + h)
+            right.append(pltpu.roll(w[f] - h, 7, 0))
+        g = twice_face(left, right, 2)
+        rho, vx, vy, vz, p, bx, by, bz = w
+        mx, my, mz = rho * vx, rho * vy, rho * vz
+        energy = (
+            p * (1.0 / (gamma_gas - 1.0))
+            + 0.5 * (mx * vx + my * vy + mz * vz)
+            + 0.5 * (bx * bx + by * by + bz * bz)
+        )
+        cons = [rho, mx, my, mz, energy, bx, by, bz]
+        src = [None] * FIELDS
+        src[1] = (time_step * 2.0 * omega_rate) * my
+        src[2] = (-time_step * (2.0 - shear_rate) * omega_rate) * mx
+        src[4] = (time_step * shear_rate * omega_rate) * (mx * vy - bx * by)
+        src[6] = (-time_step * shear_rate * omega_rate) * bx
+        for f in range(FIELDS):
+            total = cons[f] + (0.5 * time_step) * (pltpu.roll(g[f], 1, 0) - g[f])
+            acc_ref[f, x] = total if src[f] is None else total + src[f]
+        return 0
+
+    lax.fori_loop(0, nx, body, 0)
+
+
+def early():
+    return lax.axis_index("gy") == 0
+
+
+def upright_kernel(nx, wt_ref, acc_in, acc_ref):
+    @pl.when(jnp.logical_not(early()))
+    def _():
+        upright(nx, wt_ref, acc_ref)
+
+
+def pack_kernel(nx, w_ref, wt_ref, xa_ref, own_ref, ex_ref, acc_ref, sem):
+    parts = sem.shape[0]
+    copies = transposing(w_ref, wt_ref, sem, parts)
+    for part in copies:
+        for copy in part:
             copy.start()
     odd = lax.rem(lax.axis_index("gx"), 2)
     first_a = (1 - odd) * (nx - 2)
@@ -95,8 +144,9 @@
     group, place = lane // EDGE, lax.rem(lane, EDGE)
     middle = (place > 1) & (place < 6)
     for f in range(FIELDS):
-        for copy in copies[f]:
-            copy.wait()
+        if f % (FIELDS // parts) == 0:
+            for copy in copies[f // (FIELDS // parts)]:
+                copy.wait()
         for g in range(2):
             xa_ref[f, g] = wt_ref[f, first_a + g]
             ex_ref[f, g] = wt_ref[f, first_b + g]
@@ -111,8 +161,12 @@
         for v in range(0, len(tiles), 2):
             ex_ref[f, 2 + v // 2] = jnp.where(middle, tiles[v], pltpu.roll(tiles[v + 1], 4, 1))
 
-
-def shear_kernel(whole_ref, frac_ref, ex_ref, c_ref, y_ref, xb_ref):
+    @pl.when(early())
+    def _():
+        upright(nx, wt_ref, acc_ref)
+
+
+def shear_kernel(whole_ref, frac_ref, ex_ref, c_ref, y_ref, acc_ref, xb_ref):
     gx, odd_y = lax.axis_index("gx"), lax.rem(lax.axis_index("gy"), 2)
     upper = gx == lax.axis_size("gx") - 1
     end = upper | (gx == 0)
@@ -140,55 +194,26 @@
 
 
 def inner_kernel(
-    nx, wt_ref, old_ref, acc_ref, old_t, g_ref, l_ref, d_ref, al_ref, am_ref, ar_ref, ag_ref, sem
+    nx, wt_ref, up_ref, old_ref, acc_ref, old_t, g_ref, l_ref, d_ref, al_ref, am_ref, ar_ref, ag_ref, sem
 ):
-    copies = [copy for field in transposing(old_ref, old_t, sem) for copy in field]
+    copies = transposing(old_ref, old_t, sem, 1)[0]
     for copy in copies:
         copy.start()
     lane = lanes()
     whole = (lane > 0) & (lane < 126)
 
-    def finish(x, w, div):
-        rho, vx, vy, vz, p, bx, by, bz = w
-        mx, my, mz = rho * vx, rho * vy, rho * vz
-        energy = (
-            p * (1.0 / (gamma_gas - 1.0))
-            + 0.5 * (mx * vx + my * vy + mz * vz)
-            + 0.5 * (bx * bx + by * by + bz * bz)
-        )
-        cons = [rho, mx, my, mz, energy, bx, by, bz]
-        src = [None] * FIELDS
-        src[1] = (time_step * 2.0 * omega_rate) * my
-        src[2] = (-time_step * (2.0 - shear_rate) * omega_rate) * mx
-        src[4] = (time_step * shear_rate * omega_rate) * (mx * vy - bx * by)
-        src[6] = (-time_step * shear_rate * omega_rate) * bx
-        for f in range(FIELDS):
-            total = cons[f] + (0.5 * time_step) * div[f]
-            acc_ref[f, x] = total if src[f] is None else total + src[f]
-
-    def vertical(w):
-        left, right = [], []
-        for f in range(FIELDS):
-            up = pltpu.roll(w[f], 7, 0) - w[f]
-            h = half_slope(pltpu.roll(up, 1, 0), up)
-            left.append(w[f] + h)
-            right.append(pltpu.roll(w[f] - h, 7, 0))
-        g = twice_face(left, right, 2)
-        return [pltpu.roll(v, 1, 0) - v for v in g]
-
-    def radial(x):
+    def radial(x, l, d):
         w2 = rows_of(wt_ref, jnp.minimum(x + 1, nx - 1))
         w3 = rows_of(wt_ref, jnp.minimum(x + 2, nx - 1))
-        left, right = [], []
+        right, next_l, next_d = [], [], []
         for f in range(FIELDS):
             step = w3[f] - w2[f]
-            h = half_slope(d_ref[f], step)
-            left.append(l_ref[f])
+            h = half_slope(d[f], step)
             right.append(w2[f] - h)
-            l_ref[f] = w2[f] + h
-            d_ref[f] = step
+            next_l.append(w2[f] + h)
+            next_d.append(step)
         keep = jnp.where((x > 0) & (x < nx - 2), 1.0, 0.0)
-        return [keep * v for v in twice_face(left, right, 0)]
+        return [keep * v for v in twice_face(l, right, 0)], next_l, next_d
 
     def states(x):
         for f in range(FIELDS):
@@ -206,46 +231,42 @@
         for f in range(FIELDS):
             ag_ref[f, x] = jnp.where(whole, g[f], 0.0)
 
-    states(0)
-    states(1)
-    states(2)
-    turn(0)
-    turn(1)
-    faces(0)
+    for i in range(3 * UNROLL):
+        states(i)
+    for i in range(2 * UNROLL):
+        turn(i)
+    for i in range(UNROLL):
+        faces(i)
     for f in range(FIELDS):
         g_ref[f] = jnp.zeros((8, 128), jnp.float32)
         l_ref[f] = wt_ref[f, 0]
         d_ref[f] = wt_ref[f, 1] - wt_ref[f, 0]
 
-    def body(x, _):
-        w = rows_of(wt_ref, x)
-        along = rows_of(ag_ref, x)
-        along = [pltpu.roll(v, 1, 1) - v for v in along]
-        faces(jnp.minimum(x + 1, nx - 1))
-        turn(jnp.minimum(x + 2, nx - 1))
-        states(jnp.minimum(x + 3, nx - 1))
-        div = vertical(w)
-        g = radial(x)
-        for f in range(FIELDS):
-            div[f] = div[f] + (g_ref[f] - g[f]) + along[f]
-            g_ref[f] = g[f]
-        finish(x, w, div)
+    def body(i, _):
+        first = i * UNROLL
+        rows = [first + j for j in range(UNROLL)]
+        along = [[pltpu.roll(v, 1, 1) - v for v in rows_of(ag_ref, x)] for x in rows]
+        for stage, ahead in ((faces, 1), (turn, 2), (states, 3)):
+            for x in rows:
+                stage(jnp.minimum(x + ahead * UNROLL, nx - 1))
+        l, d, below = ([ref[f] for f in range(FIELDS)] for ref in (l_ref, d_ref, g_ref))
+        for x, turned in zip(rows, along):
+            g, l, d = radial(x, l, d)
+            for f in range(FIELDS):
+                div = (below[f] - g[f]) + turned[f]
+                acc_ref[f, x] = up_ref[f, x] + (0.5 * time_step) * div
+            below = g
+        for f in range(FIELDS):
+            l_ref[f], d_ref[f], g_ref[f] = l[f], d[f], below[f]
         return 0
 
-    lax.fori_loop(0, nx, body, 0)
+    lax.fori_loop(0, nx // UNROLL, body, 0)
     for copy in copies:
         copy.wait()
 
-    def add(x, _):
-        for f in range(FIELDS):
-            acc_ref[f, x] = 0.5 * (acc_ref[f, x] + old_t[f, x])
-        return 0
-
-    lax.fori_loop(0, nx, add, 0)
-
 
 def outer_kernel(
-    nx, wt_ref, acc_ref, own_ref, c_ref, y_ref, xa_ref, xb_hbm, out_ref,
+    nx, wt_ref, acc_ref, old_ref, own_ref, c_ref, y_ref, xa_ref, xb_hbm, out_ref,
     new_ref, q_ref, d_ref, xb_ref, sem, xb_sem,
 ):
     fetch = pltpu.make_async_copy(xb_hbm, xb_ref, xb_sem)
@@ -312,7 +333,7 @@
     for f in range(FIELDS):
         for x in range(nx):
             q = pltpu.roll(q_ref[f, x // ROWS], (124 - EDGE * (x % ROWS)) % 128, 1)
-            new = acc_ref[f, x] + jnp.where(edge, q, 0.0)
+            new = 0.5 * (acc_ref[f, x] + old_ref[f, x]) + jnp.where(edge, q, 0.0)
             at = {0: 0, 1: 1, nx - 2: 2, nx - 1: 3}.get(x)
             new_ref[f, x] = new if at is None else new + d_ref[f, at]
         for z in range(8):
@@ -363,18 +384,23 @@
     def room(mib):
         return pltpu.CompilerParams(vmem_limit_bytes=mib << 20)
 
+    def cost(flops):
+        n = nx * nz * cells
+        return pl.CostEstimate(flops=flops * n, bytes_accessed=12 * fields * n, transcendentals=0)
+
     w, old = (pltpu.with_memory_space_constraint(v, pltpu.HBM) for v in (section_prims, old_state))
-    wt, xa, own, ex = pl.pallas_call(
+    wt, xa, own, ex, acc = pl.pallas_call(
         functools.partial(pack_kernel, nx),
         out_shape=(
             jax.ShapeDtypeStruct(block, f32),
             edge_rows,
             jax.ShapeDtypeStruct((fields, tiles, nz, cells), f32),
             jax.ShapeDtypeStruct((fields, 2 + tiles // 2, nz, cells), f32),
+            jax.ShapeDtypeStruct(block, f32),
         ),
         in_specs=[hbm],
-        out_specs=(vmem,) * 4,
-        scratch_shapes=[pltpu.SemaphoreType.DMA((fields, nz))],
+        out_specs=(vmem,) * 5,
+        scratch_shapes=[pltpu.SemaphoreType.DMA((2, nz))],
         compiler_params=room(8),
         name="pack",
     )(w)
@@ -382,44 +408,51 @@
     c_in = lax.ppermute(ex, axes, core)
     y_in = lax.ppermute(ex, axes, cross)
     xa_in = lax.ppermute(xa, axes, along)
+    acc = pl.pallas_call(
+        functools.partial(upright_kernel, nx),
+        out_shape=jax.ShapeDtypeStruct(block, f32),
+        in_specs=[vmem, vmem],
+        out_specs=vmem,
+        input_output_aliases={1: 0},
+        compiler_params=room(8),
+        cost_estimate=cost(300),
+        name="upright",
+    )(wt, acc)
     xb = pl.pallas_call(
         shear_kernel,
         out_shape=edge_rows,
-        in_specs=[smem, smem, vmem, vmem, vmem],
+        in_specs=[smem, smem, vmem, vmem, vmem, pl.BlockSpec(memory_space=pl.ANY)],
         out_specs=vmem,
         compiler_params=room(8),
         name="shear",
-    )(shear_whole, shear_frac, ex, c_in, y_in)
+    )(shear_whole, shear_frac, ex, c_in, y_in, acc)
 
     def branch(k):
-        def run(xb, wt, old):
+        def run(xb, wt, acc, old):
             xb_in = lax.ppermute(xb, axes, other(k))
-            acc = pl.pallas_call(
+            acc, old_t = pl.pallas_call(
                 functools.partial(inner_kernel, nx),
-                out_shape=jax.ShapeDtypeStruct(block, f32),
-                in_specs=[vmem, hbm],
-                out_specs=vmem,
-                scratch_shapes=[pltpu.VMEM(block, f32)]
-                + [pltpu.VMEM(tile, f32)] * 3
+                out_shape=(jax.ShapeDtypeStruct(block, f32),) * 2,
+                in_specs=[vmem, vmem, hbm],
+                out_specs=(vmem, vmem),
+                scratch_shapes=[pltpu.VMEM(tile, f32)] * 3
                 + [pltpu.VMEM(block, f32)] * 4
-                + [pltpu.SemaphoreType.DMA((fields, nz))],
+                + [pltpu.SemaphoreType.DMA((1, nz))],
                 compiler_params=room(16),
-                cost_estimate=pl.CostEstimate(
-                    flops=720 * nx * nz * cells, bytes_accessed=12 * fields * nx * nz * cells, transcendentals=0
-                ),
+                cost_estimate=cost(480),
                 name="inner",
-            )(wt, old)
-            return xb_in, acc
+            )(wt, acc, old)
+            return xb_in, acc, old_t
 
         return run
 
     whole = lax.shift_right_logical(shear_whole[0], 7)
-    xb_in, acc = lax.switch(whole, [branch(k) for k in range(n_gy)], xb, wt, old)
+    xb_in, acc, old_t = lax.switch(whole, [branch(k) for k in range(n_gy)], xb, wt, acc, old)
 
     return pl.pallas_call(
         functools.partial(outer_kernel, nx),
         out_shape=jax.ShapeDtypeStruct(section_prims.shape, f32),
-        in_specs=[vmem] * 6 + [hbm],
+        in_specs=[vmem] * 7 + [hbm],
         out_specs=hbm,
         scratch_shapes=[
             pltpu.VMEM(block, f32),
@@ -431,7 +464,7 @@
         ],
         compiler_params=room(12),
         name="outer",
-    )(wt, acc, own, c_in, y_in, xa_in, xb_in)
+    )(wt, acc, old_t, own, c_in, y_in, xa_in, xb_in)
 
 
 def solution(mesh):

time: 21 us -> 20 us (0.952)
  the two profiles are of different devices: /device:TPU:0 before, /device:TPU:6 now
where the time goes in v1:
time: 20 us
  Pallas kernels  8.92 us (45%)
  waiting for transfers between devices  5.19 us (26%)
  starting transfers between devices  4.56 us (23%)
  between operations  1.33 us (7%)
    pallas_call x1, Pallas kernels, on_device(): pl.pallas_call(functools.partial(pack_kernel, nx), out_shape=(jax.ShapeDt...  3.29 us
    pallas_call x1, Pallas kernels, run(): pl.pallas_call(functools.partial(inner_kernel, nx), out_shape=(jax.ShapeD...  2.86 us
    ppermute x1, waiting for transfers between devices, run(): xb_in = lax.ppermute(xb, axes, other(k))  2.7 us
    pallas_call x1, Pallas kernels, on_device(): pl.pallas_call(functools.partial(outer_kernel, nx), out_shape=jax.ShapeDt...  2.6 us
    ppermute x1, waiting for transfers between devices, on_device(): y_in = lax.ppermute(ex, axes, cross)  2.48 us
    ppermute x1, starting transfers between devices, run(): xb_in = lax.ppermute(xb, axes, other(k))  2.46 us
    ppermute x1, starting transfers between devices, on_device(): y_in = lax.ppermute(ex, axes, cross)  1.56 us
    ppermute x1, starting transfers between devices, on_device(): xa_in = lax.ppermute(xa, axes, along)  0.54 us
  transfers between devices with their start and end apart: 4, of which 2 were waited for; matrix products, arithmetic and copies ran while one was open for 0% of the time, Pallas kernels for 15%

profile of v1, /device:TPU:6, one launch (start us, length us, event | category | flops | bytes accessed | tf_op | source)
XLA Modules:
  0.0 20.0 jit_solution(16527954743889828291)
XLA Ops:
  0.0 3.3 %pack.1 = (f32[8,32,8,128]{3,2,1,0:T(8,128)S(1)}, f32[8,2,8,128]{3,2,1,0:T(8,128)S(1)}, f32[8,2,8,128]{3,2,1,0:T(8,128)S(1)}, f32[8,3,8,128]{3,2,1,0:T(8,128)S(1)}, f32[8,32,8,128]{3,2,1,0:T(8,128)S(1)}) custom-call(f32[8,8,32,128]{3,2,1,0:T(8,128)} %w_ref.1), custom_call_target="tpu_custom_call" | custom-call | tf_op jit(solution)/shard_map/pack/pallas_call | solution.py:392
  3.3 1.6 %collective-permute-start.9 = (f32[8,3,8,128]{3,2,1,0:T(8,128)S(1)}, f32[8,3,8,128]{3,2,1,0:T(8,128)S(1)}, u32[]{:S(2)}, u32[]{:S(2)}) collective-permute-start(f32[8,3,8,128]{3,2,1,0:T(8,128)S(1)} %get-tuple-element.126.ex_ref), channel_id=1, source_target_pairs={{0,7},{1,2},{2,1},{3,4},{4,3},{5,6},{6,5},{7,0},{8,15},{9,10},{10,... | collective-permute-start | bytes 294920 | tf_op jit(solution)/shard_map/ppermute | solution.py:409
  4.9 0.0 collective-permute-start.8
  4.9 0.5 %collective-permute-start.10 = (f32[8,2,8,128]{3,2,1,0:T(8,128)S(1)}, f32[8,2,8,128]{3,2,1,0:T(8,128)S(1)}, u32[]{:S(2)}, u32[]{:S(2)}) collective-permute-start(f32[8,2,8,128]{3,2,1,0:T(8,128)S(1)} %get-tuple-element.131), channel_id=1, source_target_pairs={{0,8},{1,9},{2,10},{3,11},{4,12},{5,13},{6,14},{7,15},{8,0},{9,1},... | collective-permute-start | bytes 196616 | tf_op jit(solution)/shard_map/ppermute | solution.py:410
  6.7 2.5 %collective-permute-done.9.y_ref = f32[8,3,8,128]{3,2,1,0:T(8,128)S(1)} collective-permute-done((f32[8,3,8,128]{3,2,1,0:T(8,128)S(1)}, f32[8,3,8,128]{3,2,1,0:T(8,128)S(1)}, u32[]{:S(2)}, u32[]{:S(2)}) %collective-permute-start.9) | collective-permute-done | bytes 98336 | tf_op jit(solution)/shard_map/ppermute | solution.py:409
  9.2 0.0 collective-permute-done.8.c_ref
  9.2 0.1 shear.1
  9.4 8.1 %conditional.1 = (f32[8,2,8,128]{3,2,1,0:T(8,128)}, f32[8,32,8,128]{3,2,1,0:T(8,128)S(1)}, f32[8,32,8,128]{3,2,1,0:T(8,128)S(1)}) conditional(s32[]{:T(128)} %bitcast, (f32[8,2,8,128]{3,2,1,0:T(8,128)S(1)}, f32[8,32,8,128]{3,2,1,0:T(8,128)S(1)}, f32[8,32,8,128]{3,2,1,0:T(8,128)S(1)}, ...), branch_computations={%region_0.0_spmd, %region_1.0_spmd, %region_2.0_spmd, %region_3.0_... | conditional | flops 15728640 | bytes 3407936 | solution.py:450
  9.4 2.5 %collective-permute-start.2 = (f32[8,2,8,128]{3,2,1,0:T(8,128)S(1)}, f32[8,2,8,128]{3,2,1,0:T(8,128)}, u32[]{:S(2)}, u32[]{:S(2)}) collective-permute-start(f32[8,2,8,128]{3,2,1,0:T(8,128)S(1)} %get-tuple-element.81), channel_id=1, source_target_pairs={{8,16},{9,17},{10,18},{11,19},{12,20},{13,21},{14,22},{15,23},{16,... | collective-permute-start | bytes 196616 | tf_op jit(solution)/shard_map/cond/branch_2_fun/ppermute | solution.py:432
  11.9 2.9 %inner.10 = (f32[8,32,8,128]{3,2,1,0:T(8,128)S(1)}, f32[8,32,8,128]{3,2,1,0:T(8,128)S(1)}) custom-call(f32[8,32,8,128]{3,2,1,0:T(8,128)S(1)} %get-tuple-element.82.wt_ref, f32[8,32,8,128]{3,2,1,0:T(8,128)S(1)} %get-tuple-element.83.up_ref, f32[8,8,32,128]{3,2,1,0:T(8,128)} %get-tuple-element.84.old_ref), custom_call_target="tpu_custom_call" | custom-call | flops 15728640 | bytes 3145728 | tf_op jit(solution)/shard_map/cond/branch_2_fun/inner/pallas_call | solution.py:433
  14.7 2.7 %collective-permute-done.2 = f32[8,2,8,128]{3,2,1,0:T(8,128)} collective-permute-done((f32[8,2,8,128]{3,2,1,0:T(8,128)S(1)}, f32[8,2,8,128]{3,2,1,0:T(8,128)}, u32[]{:S(2)}, u32[]{:S(2)}) %collective-permute-start.2) | collective-permute-done | bytes 65568 | tf_op jit(solution)/shard_map/cond/branch_2_fun/ppermute | solution.py:432
  17.4 0.0 collective-permute-done.10.xa_ref
  17.4 2.6 %outer.1 = f32[8,8,32,128]{3,2,1,0:T(8,128)} custom-call(f32[8,32,8,128]{3,2,1,0:T(8,128)S(1)} %get-tuple-element.125.wt_ref, f32[8,32,8,128]{3,2,1,0:T(8,128)S(1)} %get-tuple-element.128.acc_ref, f32[8,32,8,128]{3,2,1,0:T(8,128)S(1)} %get-tuple-element.129.old_ref, f32[8,2,8,128]{3,2,1,0:T(8,128)S(1)} %get-tuple-element.130.own_ref, ...), custom_call_target="tpu_custom_call" | custom-call | tf_op jit(solution)/shard_map/outer/pallas_call | solution.py:452
  (1 shorter events, 0.0 us)
Async XLA Ops:
  3.3 5.9 %collective-permute-start.9 = (f32[8,3,8,128]{3,2,1,0:T(8,128)S(1)}, f32[8,3,8,128]{3,2,1,0:T(8,128)S(1)}, u32[]{:S(2)}, u32[]{:S(2)}) collective-permute-start(f32[8,3,8,128]{3,2,1,0:T(8,128)S(1)} %get-tuple-element.126.ex_ref), channel_id=1, source_target_pairs={{0,7},{1,2},{2,1},{3,4},{4,3},{5,6},{6,5},{7,0},{8,15},{9,10},{10,... | collective-permute-start | bytes 294920 | tf_op jit(solution)/shard_map/ppermute | solution.py:409
  4.9 4.4 %collective-permute-start.8 = (f32[8,3,8,128]{3,2,1,0:T(8,128)S(1)}, f32[8,3,8,128]{3,2,1,0:T(8,128)S(1)}, u32[]{:S(2)}, u32[]{:S(2)}) collective-permute-start(f32[8,3,8,128]{3,2,1,0:T(8,128)S(1)} %get-tuple-element.126.ex_ref), channel_id=1, source_target_pairs={{0,1},{1,0},{2,3},{3,2},{4,5},{5,4},{6,7},{7,6},{8,9},{9,8},{10,11... | collective-permute-start | bytes 294920 | tf_op jit(solution)/shard_map/ppermute | solution.py:408
  4.9 12.6 %collective-permute-start.10 = (f32[8,2,8,128]{3,2,1,0:T(8,128)S(1)}, f32[8,2,8,128]{3,2,1,0:T(8,128)S(1)}, u32[]{:S(2)}, u32[]{:S(2)}) collective-permute-start(f32[8,2,8,128]{3,2,1,0:T(8,128)S(1)} %get-tuple-element.131), channel_id=1, source_target_pairs={{0,8},{1,9},{2,10},{3,11},{4,12},{5,13},{6,14},{7,15},{8,0},{9,1},... | collective-permute-start | bytes 196616 | tf_op jit(solution)/shard_map/ppermute | solution.py:410
  9.4 8.0 %collective-permute-start.2 = (f32[8,2,8,128]{3,2,1,0:T(8,128)S(1)}, f32[8,2,8,128]{3,2,1,0:T(8,128)}, u32[]{:S(2)}, u32[]{:S(2)}) collective-permute-start(f32[8,2,8,128]{3,2,1,0:T(8,128)S(1)} %get-tuple-element.81), channel_id=1, source_target_pairs={{8,16},{9,17},{10,18},{11,19},{12,20},{13,21},{14,22},{15,23},{16,... | collective-permute-start | bytes 196616 | tf_op jit(solution)/shard_map/cond/branch_2_fun/ppermute | solution.py:432

commit v2 on v1

--- a/solution.py
+++ b/solution.py
@@ -122,7 +122,7 @@
 
 
 def early():
-    return lax.axis_index("gy") == 0
+    return (lax.axis_index("gx") == 0) & (lax.axis_index("gy") < 2)
 
 
 def upright_kernel(nx, wt_ref, acc_in, acc_ref):
@@ -194,7 +194,8 @@
 
 
 def inner_kernel(
-    nx, wt_ref, up_ref, old_ref, acc_ref, old_t, g_ref, l_ref, d_ref, al_ref, am_ref, ar_ref, ag_ref, sem
+    nx, wt_ref, up_ref, old_ref, own_ref, c_ref, y_ref, out_ref, edge_ref,
+    acc_ref, old_t, new_ref, q_ref, g_ref, l_ref, d_ref, al_ref, am_ref, ar_ref, ag_ref, sem, out_sem,
 ):
     copies = transposing(old_ref, old_t, sem, 1)[0]
     for copy in copies:
@@ -261,20 +262,8 @@
         return 0
 
     lax.fori_loop(0, nx // UNROLL, body, 0)
-    for copy in copies:
-        copy.wait()
-
-
-def outer_kernel(
-    nx, wt_ref, acc_ref, old_ref, own_ref, c_ref, y_ref, xa_ref, xb_hbm, out_ref,
-    new_ref, q_ref, d_ref, xb_ref, sem, xb_sem,
-):
-    fetch = pltpu.make_async_copy(xb_hbm, xb_ref, xb_sem)
-    fetch.start()
-    odd_x, odd_y = lax.rem(lax.axis_index("gx"), 2), lax.rem(lax.axis_index("gy"), 2)
-    lane = lanes()
+    odd_y = lax.rem(lax.axis_index("gy"), 2)
     scale = 0.25 * time_step
-
     place = lax.rem(lane, EDGE)
     low = place < 4
     for v in range(nx // ROWS):
@@ -300,14 +289,51 @@
             upper = jnp.where(low, g[f], jnp.where(place == 4, pltpu.roll(g[f], 127, 1), 0.0))
             q_ref[f, v] = scale * (lower - upper)
 
-    fetch.wait()
+    for copy in copies:
+        copy.wait()
+    ends = (lane < 2) | (lane > 125)
+    parts = out_sem.shape[0]
+    copies = []
+    for f in range(FIELDS):
+        for x in range(nx):
+            q = pltpu.roll(q_ref[f, x // ROWS], (124 - EDGE * (x % ROWS)) % 128, 1)
+            new = 0.5 * (acc_ref[f, x] + old_t[f, x]) + jnp.where(ends, q, 0.0)
+            if x < 8:
+                edge_ref[f, x] = new
+            elif x >= nx - 8:
+                edge_ref[f, x - nx + 16] = new
+            else:
+                new_ref[f, x - 8] = new
+        if (f + 1) % (FIELDS // parts) == 0:
+            part = (f + 1) // (FIELDS // parts) - 1
+            span = slice(f + 1 - FIELDS // parts, f + 1)
+            for z in range(8):
+                copy = pltpu.make_async_copy(
+                    new_ref.at[span, :, z], out_ref.at[span, z, 8 : nx - 8], out_sem.at[part, z]
+                )
+                copy.start()
+                copies.append(copy)
+    for copy in copies:
+        copy.wait()
+
+
+def outer_kernel(
+    nx, wt_ref, edge_ref, xa_ref, xb_hbm, part_ref, out_ref, new_ref, xb_ref, sem, xb_sem
+):
+    fetch = pltpu.make_async_copy(xb_hbm, xb_ref, xb_sem)
+    fetch.start()
+    odd_x = lax.rem(lax.axis_index("gx"), 2)
+    scale = 0.25 * time_step
+    for f in range(FIELDS):
+        for i in range(16):
+            new_ref[f, i] = edge_ref[f, i]
+
+    def rows(x):
+        return rows_of(wt_ref, x)
 
     def ghosts(i):
         above = (odd_x == 1) != (i < 2)
         return [jnp.where(above, xb_ref[f, i % 2], xa_ref[f, i % 2]) for f in range(FIELDS)]
-
-    def rows(x):
-        return rows_of(wt_ref, x)
 
     def radial(w0, w1, w2, w3):
         left, right = [], []
@@ -317,30 +343,33 @@
             right.append(w2[f] - half_slope(mid, w3[f] - w2[f]))
         return twice_face(left, right, 0)
 
+    def send(i):
+        first = (nx - 8) * i
+        return [
+            pltpu.make_async_copy(
+                new_ref.at[:, 8 * i : 8 * i + 8, z], out_ref.at[:, z, first : first + 8], sem.at[i, z]
+            )
+            for z in range(8)
+        ]
+
+    fetch.wait()
     g0 = radial(ghosts(0), ghosts(1), rows(0), rows(1))
     g1 = radial(ghosts(1), rows(0), rows(1), rows(2))
     for f in range(FIELDS):
-        d_ref[f, 0] = scale * (g0[f] - g1[f])
-        d_ref[f, 1] = scale * g1[f]
+        new_ref[f, 0] = edge_ref[f, 0] + scale * (g0[f] - g1[f])
+        new_ref[f, 1] = edge_ref[f, 1] + scale * g1[f]
+    copies = send(0)
+    for copy in copies:
+        copy.start()
     g0 = radial(rows(nx - 3), rows(nx - 2), rows(nx - 1), ghosts(2))
     g1 = radial(rows(nx - 2), rows(nx - 1), ghosts(2), ghosts(3))
     for f in range(FIELDS):
-        d_ref[f, 2] = -scale * g0[f]
-        d_ref[f, 3] = scale * (g0[f] - g1[f])
-
-    edge = (lane < 2) | (lane > 125)
-    copies = []
-    for f in range(FIELDS):
-        for x in range(nx):
-            q = pltpu.roll(q_ref[f, x // ROWS], (124 - EDGE * (x % ROWS)) % 128, 1)
-            new = 0.5 * (acc_ref[f, x] + old_ref[f, x]) + jnp.where(edge, q, 0.0)
-            at = {0: 0, 1: 1, nx - 2: 2, nx - 1: 3}.get(x)
-            new_ref[f, x] = new if at is None else new + d_ref[f, at]
-        for z in range(8):
-            copy = pltpu.make_async_copy(new_ref.at[f, :, z], out_ref.at[f, z], sem.at[f, z])
-            copy.start()
-            copies.append(copy)
-    for copy in copies:
+        new_ref[f, 14] = edge_ref[f, 14] - scale * g0[f]
+        new_ref[f, 15] = edge_ref[f, 15] + scale * (g0[f] - g1[f])
+    more = send(1)
+    for copy in more:
+        copy.start()
+    for copy in copies + more:
         copy.wait()
 
 
@@ -428,43 +457,49 @@
     )(shear_whole, shear_frac, ex, c_in, y_in, acc)
 
     def branch(k):
-        def run(xb, wt, acc, old):
+        def run(xb, wt, acc, old, own, c_in, y_in):
             xb_in = lax.ppermute(xb, axes, other(k))
-            acc, old_t = pl.pallas_call(
+            out, edge = pl.pallas_call(
                 functools.partial(inner_kernel, nx),
-                out_shape=(jax.ShapeDtypeStruct(block, f32),) * 2,
-                in_specs=[vmem, vmem, hbm],
-                out_specs=(vmem, vmem),
-                scratch_shapes=[pltpu.VMEM(tile, f32)] * 3
+                out_shape=(
+                    jax.ShapeDtypeStruct(section_prims.shape, f32),
+                    jax.ShapeDtypeStruct((fields, 16, nz, cells), f32),
+                ),
+                in_specs=[vmem, vmem, hbm, vmem, vmem, vmem],
+                out_specs=(hbm, vmem),
+                scratch_shapes=[pltpu.VMEM(block, f32)] * 2
+                + [pltpu.VMEM((fields, nx - 16, nz, cells), f32)]
+                + [pltpu.VMEM((fields, tiles, nz, cells), f32)]
+                + [pltpu.VMEM(tile, f32)] * 3
                 + [pltpu.VMEM(block, f32)] * 4
-                + [pltpu.SemaphoreType.DMA((1, nz))],
+                + [pltpu.SemaphoreType.DMA((1, nz)), pltpu.SemaphoreType.DMA((2, nz))],
                 compiler_params=room(16),
                 cost_estimate=cost(480),
                 name="inner",
-            )(wt, acc, old)
-            return xb_in, acc, old_t
+            )(wt, acc, old, own, c_in, y_in)
+            return xb_in, out, edge
 
         return run
 
     whole = lax.shift_right_logical(shear_whole[0], 7)
-    xb_in, acc, old_t = lax.switch(whole, [branch(k) for k in range(n_gy)], xb, wt, acc, old)
-
+    xb_in, out, edge = lax.switch(
+        whole, [branch(k) for k in range(n_gy)], xb, wt, acc, old, own, c_in, y_in
+    )
     return pl.pallas_call(
         functools.partial(outer_kernel, nx),
         out_shape=jax.ShapeDtypeStruct(section_prims.shape, f32),
-        in_specs=[vmem] * 7 + [hbm],
+        in_specs=[vmem] * 3 + [hbm, hbm],
         out_specs=hbm,
+        input_output_aliases={4: 0},
         scratch_shapes=[
-            pltpu.VMEM(block, f32),
-            pltpu.VMEM((fields, tiles, nz, cells), f32),
-            pltpu.VMEM((fields, 4, nz, cells), f32),
+            pltpu.VMEM((fields, 16, nz, cells), f32),
             pltpu.VMEM((fields, 2, nz, cells), f32),
-            pltpu.SemaphoreType.DMA((fields, nz)),
+            pltpu.SemaphoreType.DMA((2, nz)),
             pltpu.SemaphoreType.DMA,
         ],
-        compiler_params=room(12),
+        compiler_params=room(8),
         name="outer",
-    )(wt, acc, old_t, own, c_in, y_in, xa_in, xb_in)
+    )(wt, edge, xa_in, xb_in, out)
 
 
 def solution(mesh):

time: 20 us -> 19.7 us (0.985)
  the two profiles are of different devices: /device:TPU:6 before, /device:TPU:0 now
where the time goes in v2:
time: 19.7 us; the launch traced here: 19.9 us
  Pallas kernels  9.65 us (49%)
  starting transfers between devices  7.43 us (38%)
  waiting for transfers between devices  1.44 us (7%)
  between operations  1.33 us (7%)
    pallas_call x1, Pallas kernels, run(): pl.pallas_call(functools.partial(inner_kernel, nx), out_shape=(jax.ShapeD...  4.33 us
    pallas_call x1, Pallas kernels, on_device(): pl.pallas_call(functools.partial(pack_kernel, nx), out_shape=(jax.ShapeDt...  3.29 us
    ppermute x1, starting transfers between devices, on_device(): y_in = lax.ppermute(ex, axes, cross)  3.01 us
    ppermute x1, starting transfers between devices, run(): xb_in = lax.ppermute(xb, axes, other(k))  2.93 us
    pallas_call x1, Pallas kernels, on_device(): pl.pallas_call(functools.partial(outer_kernel, nx), out_shape=jax.ShapeDt...  1.86 us
    ppermute x1, starting transfers between devices, on_device(): xa_in = lax.ppermute(xa, axes, along)  1.49 us
    ppermute x1, waiting for transfers between devices, on_device(): y_in = lax.ppermute(ex, axes, cross)  0.87 us
    ppermute x1, waiting for transfers between devices, run(): xb_in = lax.ppermute(xb, axes, other(k))  0.57 us
  transfers between devices with their start and end apart: 4, of which 2 were waited for; matrix products, arithmetic and copies ran while one was open for 0% of the time, Pallas kernels for 23%

profile of v2, /device:TPU:0, one launch (start us, length us, event | category | flops | bytes accessed | tf_op | source)
XLA Modules:
  0.0 19.9 jit_solution(10442053310957941106)
XLA Ops:
  0.0 3.3 %pack.1 = (f32[8,32,8,128]{3,2,1,0:T(8,128)S(1)}, f32[8,2,8,128]{3,2,1,0:T(8,128)S(1)}, f32[8,2,8,128]{3,2,1,0:T(8,128)S(1)}, f32[8,3,8,128]{3,2,1,0:T(8,128)S(1)}, f32[8,32,8,128]{3,2,1,0:T(8,128)S(1)}) custom-call(f32[8,8,32,128]{3,2,1,0:T(8,128)} %w_ref.1), custom_call_target="tpu_custom_call" | custom-call | tf_op jit(solution)/shard_map/pack/pallas_call | solution.py:421
  3.3 3.0 %collective-permute-start.9 = (f32[8,3,8,128]{3,2,1,0:T(8,128)S(1)}, f32[8,3,8,128]{3,2,1,0:T(8,128)S(1)}, u32[]{:S(2)}, u32[]{:S(2)}) collective-permute-start(f32[8,3,8,128]{3,2,1,0:T(8,128)S(1)} %get-tuple-element.198.ex_ref), channel_id=1, source_target_pairs={{0,7},{1,2},{2,1},{3,4},{4,3},{5,6},{6,5},{7,0},{8,15},{9,10},{10,... | collective-permute-start | bytes 294920 | tf_op jit(solution)/shard_map/ppermute | solution.py:438
  6.3 0.0 collective-permute-start.8
  6.3 1.5 %collective-permute-start.10 = (f32[8,2,8,128]{3,2,1,0:T(8,128)S(1)}, f32[8,2,8,128]{3,2,1,0:T(8,128)S(1)}, u32[]{:S(2)}, u32[]{:S(2)}) collective-permute-start(f32[8,2,8,128]{3,2,1,0:T(8,128)S(1)} %get-tuple-element.202), channel_id=1, source_target_pairs={{0,8},{1,9},{2,10},{3,11},{4,12},{5,13},{6,14},{7,15},{8,0},{9,1},... | collective-permute-start | bytes 196616 | tf_op jit(solution)/shard_map/ppermute | solution.py:439
  9.1 0.9 %collective-permute-done.9.y_ref = f32[8,3,8,128]{3,2,1,0:T(8,128)S(1)} collective-permute-done((f32[8,3,8,128]{3,2,1,0:T(8,128)S(1)}, f32[8,3,8,128]{3,2,1,0:T(8,128)S(1)}, u32[]{:S(2)}, u32[]{:S(2)}) %collective-permute-start.9) | collective-permute-done | bytes 98336 | tf_op jit(solution)/shard_map/ppermute | solution.py:438
  10.0 0.0 collective-permute-done.8.c_ref
  10.0 0.1 shear.1
  10.2 7.9 %conditional.1 = (f32[8,2,8,128]{3,2,1,0:T(8,128)}, f32[8,8,32,128]{3,2,1,0:T(8,128)}, f32[8,16,8,128]{3,2,1,0:T(8,128)S(1)}) conditional(s32[]{:T(128)} %bitcast, (f32[8,2,8,128]{3,2,1,0:T(8,128)S(1)}, f32[8,32,8,128]{3,2,1,0:T(8,128)S(1)}, f32[8,32,8,128]{3,2,1,0:T(8,128)S(1)}, f32[8,8,32,128]{3,2,1,0:T(8,128)}, ...), branch_computations={%region_0.0_spmd, %region_1.0_spmd, %region_2.0_spmd, %region_3.0_... | conditional | flops 15728640 | bytes 3407936 | solution.py:485
  10.2 2.9 %collective-permute-start.4 = (f32[8,2,8,128]{3,2,1,0:T(8,128)S(1)}, f32[8,2,8,128]{3,2,1,0:T(8,128)}, u32[]{:S(2)}, u32[]{:S(2)}) collective-permute-start(f32[8,2,8,128]{3,2,1,0:T(8,128)S(1)} %get-tuple-element.153), channel_id=1, source_target_pairs={{8,16},{9,17},{10,18},{11,19},{12,20},{13,21},{14,22},{15,23},{16,... | collective-permute-start | bytes 196616 | tf_op jit(solution)/shard_map/cond/branch_4_fun/ppermute | solution.py:461
  13.1 4.3 %inner.12 = (f32[8,8,32,128]{3,2,1,0:T(8,128)}, f32[8,16,8,128]{3,2,1,0:T(8,128)S(1)}) custom-call(f32[8,32,8,128]{3,2,1,0:T(8,128)S(1)} %get-tuple-element.154.wt_ref, f32[8,32,8,128]{3,2,1,0:T(8,128)S(1)} %get-tuple-element.155.up_ref, f32[8,8,32,128]{3,2,1,0:T(8,128)} %get-tuple-element.156.old_ref, f32[8,2,8,128]{3,2,1,0:T(8,128)S(1)} %get-tuple-element.157.own_ref, ...), custom_call_target="tpu_custom_call" | custom-call | flops 15728640 | bytes 3145728 | tf_op jit(solution)/shard_map/cond/branch_4_fun/inner/pallas_call | solution.py:462
  17.5 0.6 %collective-permute-done.4 = f32[8,2,8,128]{3,2,1,0:T(8,128)} collective-permute-done((f32[8,2,8,128]{3,2,1,0:T(8,128)S(1)}, f32[8,2,8,128]{3,2,1,0:T(8,128)}, u32[]{:S(2)}, u32[]{:S(2)}) %collective-permute-start.4) | collective-permute-done | bytes 65568 | tf_op jit(solution)/shard_map/cond/branch_4_fun/ppermute | solution.py:461
  18.0 0.0 collective-permute-done.10.xa_ref
  18.0 1.9 %outer.1 = f32[8,8,32,128]{3,2,1,0:T(8,128)} custom-call(f32[8,32,8,128]{3,2,1,0:T(8,128)S(1)} %get-tuple-element.197.wt_ref, f32[8,16,8,128]{3,2,1,0:T(8,128)S(1)} %get-tuple-element.201.edge_ref, f32[8,2,8,128]{3,2,1,0:T(8,128)S(1)} %collective-permute-done.10.xa_ref, f32[8,2,8,128]{3,2,1,0:T(8,128)} %get-tuple-element.203.xb_hbm, ...), custom_call_target="tpu_custom_call", output_to_operand_aliasing={{}: (4, {})} | custom-call | tf_op jit(solution)/shard_map/outer/pallas_call | solution.py:488
  (1 shorter events, 0.0 us)
Async XLA Ops:
  3.3 6.7 %collective-permute-start.9 = (f32[8,3,8,128]{3,2,1,0:T(8,128)S(1)}, f32[8,3,8,128]{3,2,1,0:T(8,128)S(1)}, u32[]{:S(2)}, u32[]{:S(2)}) collective-permute-start(f32[8,3,8,128]{3,2,1,0:T(8,128)S(1)} %get-tuple-element.198.ex_ref), channel_id=1, source_target_pairs={{0,7},{1,2},{2,1},{3,4},{4,3},{5,6},{6,5},{7,0},{8,15},{9,10},{10,... | collective-permute-start | bytes 294920 | tf_op jit(solution)/shard_map/ppermute | solution.py:438
  6.3 3.7 %collective-permute-start.8 = (f32[8,3,8,128]{3,2,1,0:T(8,128)S(1)}, f32[8,3,8,128]{3,2,1,0:T(8,128)S(1)}, u32[]{:S(2)}, u32[]{:S(2)}) collective-permute-start(f32[8,3,8,128]{3,2,1,0:T(8,128)S(1)} %get-tuple-element.198.ex_ref), channel_id=1, source_target_pairs={{0,1},{1,0},{2,3},{3,2},{4,5},{5,4},{6,7},{7,6},{8,9},{9,8},{10,11... | collective-permute-start | bytes 294920 | tf_op jit(solution)/shard_map/ppermute | solution.py:437
  6.3 11.7 %collective-permute-start.10 = (f32[8,2,8,128]{3,2,1,0:T(8,128)S(1)}, f32[8,2,8,128]{3,2,1,0:T(8,128)S(1)}, u32[]{:S(2)}, u32[]{:S(2)}) collective-permute-start(f32[8,2,8,128]{3,2,1,0:T(8,128)S(1)} %get-tuple-element.202), channel_id=1, source_target_pairs={{0,8},{1,9},{2,10},{3,11},{4,12},{5,13},{6,14},{7,15},{8,0},{9,1},... | collective-permute-start | bytes 196616 | tf_op jit(solution)/shard_map/ppermute | solution.py:439
  10.2 7.8 %collective-permute-start.4 = (f32[8,2,8,128]{3,2,1,0:T(8,128)S(1)}, f32[8,2,8,128]{3,2,1,0:T(8,128)}, u32[]{:S(2)}, u32[]{:S(2)}) collective-permute-start(f32[8,2,8,128]{3,2,1,0:T(8,128)S(1)} %get-tuple-element.153), channel_id=1, source_target_pairs={{8,16},{9,17},{10,18},{11,19},{12,20},{13,21},{14,22},{15,23},{16,... | collective-permute-start | bytes 196616 | tf_op jit(solution)/shard_map/cond/branch_4_fun/ppermute | solution.py:461
